TPU v7x, 256 devices: a whole 4x4x8 slice. The times are simulated.
256 devices in a mesh: group: 8 (over z_lo, y), dev: 32 (over z_hi, x, core).
Axes of the slice: x: 4, y: 4, z: 8 (z_hi: 4, z_lo: 2; z = z_hi * 2 + z_lo), core: 2. Of those that a mesh axis runs over, the one named last changes fastest.
Arguments:
- right_side: float32 [3, 16, 64, 64, 128], P(None, 'group', 'dev'), may hold values from -60 to 60
- stiff_diag: float32 [3, 3, 16, 4096], P(None, None, 'group', 'dev'), may hold values from -0.1 to 12.75, as said below
- stiff_lower: float32 [3, 3, 13, 16, 4096], P(None, None, None, 'group', 'dev'), may hold values from -0.08 to 0.08
- fsai_diag: float32 [3, 3, 16, 4096], P(None, None, 'group', 'dev'), may hold values from -0.1 to 1, as said below
- fsai_lower: float32 [3, 3, 13, 16, 4096], P(None, None, None, 'group', 'dev'), may hold values from -0.12 to 0.12
- fsai_pattern: int32 [13, 16, 4096], P(None, 'group', 'dev'), may hold values 0 or 1
Outputs:
- solution: float32 [3, 16, 64, 64, 128], P(None, 'group', 'dev')
- residual: float32 [3, 16, 64, 64, 128], P(None, 'group', 'dev')
Inputs may be any that keep to these rules, and one draw needn't show every extreme that they name: `stiff_diag`: each 3 by 3 block is symmetric. `fsai_diag`: each 3 by 3 block is zero above its diagonal and positive on it.
All inputs are finite; a program needn't handle non-finite values. No bound on the sum of `fsai_pattern` on one device may be relied on, other than what follows from the above.
Results may differ from a plain program's by a relative error of at most 0.0003.
Values sent between devices are 32-bit elements; how exact they have to be, the bound alone decides.
A program may use at most 128 MiB of HBM per device.

v0:
```python
import jax
import jax.numpy as jnp
from jax import lax
from jax.sharding import PartitionSpec as P

ITERS = 2
highest = lax.Precision.HIGHEST
lower_offsets = [(0, 0, -1), (0, -1, -1), (0, -1, 0), (0, -1, 1)] + [
    (-1, row_step, column_step) for row_step in (-1, 0, 1) for column_step in (-1, 0, 1)
]


def with_halo(block, sides, width):
    for axis, dim in sides:
        count = lax.axis_size(axis)
        forward = [(i, i + 1) for i in range(count - 1)]
        backward = [(target, source) for source, target in forward]
        low = lax.ppermute(
            lax.slice_in_dim(block, block.shape[dim] - width, None, axis=dim), axis, forward
        )
        high = lax.ppermute(lax.slice_in_dim(block, 0, width, axis=dim), axis, backward)
        block = jnp.concatenate([low, block, high], axis=dim)
    return block


def from_behind(value, axis, steps):
    count = lax.axis_size(axis)
    first, last = (max(0, -steps), min(count, count - steps))
    return lax.ppermute(value, axis, [(source, source + steps) for source in range(first, last)])


def block_mul(coeffs, vector):
    return jnp.stack(
        [
            coeffs[target, 0][..., None] * vector[0]
            + coeffs[target, 1][..., None] * vector[1]
            + coeffs[target, 2][..., None] * vector[2]
            for target in range(3)
        ]
    )


def block_mul_transposed(coeffs, vector):
    return jnp.stack(
        [
            coeffs[0, target][..., None] * vector[0]
            + coeffs[1, target][..., None] * vector[1]
            + coeffs[2, target][..., None] * vector[2]
            for target in range(3)
        ]
    )


def pad_columns(vector):
    return jnp.pad(vector, ((0, 0), (0, 0), (0, 0), (1, 1), (0, 0)))


def local_gram(left_block, right_block):
    return jnp.einsum("azxyr,azxys->rs", left_block, right_block, precision=highest)


def combine(vector, coeffs):
    return jnp.einsum("azxyr,rs->azxys", vector, coeffs, precision=highest)


def gram_solve(matrix, right_terms):
    factor = jnp.linalg.cholesky(matrix)
    halfway = lax.linalg.triangular_solve(factor, right_terms, left_side=True, lower=True)
    return lax.linalg.triangular_solve(
        factor, halfway, left_side=True, lower=True, transpose_a=True
    )


def per_device(right_side, stiff_diag, stiff_lower, fsai_diag, fsai_lower, fsai_pattern):
    local_planes = right_side.shape[1]
    local_rows = right_side.shape[2]
    line_length = right_side.shape[3]
    slot_count = stiff_lower.shape[2]
    stiff_d = stiff_diag.reshape(3, 3, local_planes, local_rows, line_length)
    fsai_d = fsai_diag.reshape(3, 3, local_planes, local_rows, line_length)
    stiff_low = stiff_lower.reshape(3, 3, slot_count, local_planes, local_rows, line_length)
    kept = fsai_pattern.astype(jnp.float32)
    fsai_low = (fsai_lower * kept[None, None]).reshape(
        3, 3, slot_count, local_planes, local_rows, line_length
    )

    def lower_window(vector):
        rimmed = with_halo(vector, (("dev", 2),), 1)
        plane_under = from_behind(rimmed[:, local_planes - 1 :], "group", 1)
        return pad_columns(jnp.concatenate([plane_under, rimmed], axis=1))

    def gather_lower(diag_blocks, low_blocks, window_data, vector):
        result = block_mul(diag_blocks, vector)
        for slot_index, (depth_step, row_step, column_step) in enumerate(lower_offsets):
            picked = window_data[
                :,
                1 + depth_step : 1 + depth_step + local_planes,
                1 + row_step : 1 + row_step + local_rows,
                1 + column_step : 1 + column_step + line_length,
            ]
            result = result + block_mul(low_blocks[:, :, slot_index], picked)
        return result

    def push_upper(low_blocks, vector):
        buffer = None
        for slot_index, (depth_step, row_step, column_step) in enumerate(lower_offsets):
            slot_term = block_mul_transposed(low_blocks[:, :, slot_index], vector)
            placed = jnp.pad(
                slot_term,
                (
                    (0, 0),
                    (1 + depth_step, -depth_step),
                    (1 + row_step, 1 - row_step),
                    (1 + column_step, 1 - column_step),
                    (0, 0),
                ),
            )
            buffer = placed if buffer is None else buffer + placed
        inner_part = buffer[:, :, :, 1 : line_length + 1]
        rim_rows = jnp.concatenate(
            [inner_part[:, :, :1], inner_part[:, :, local_rows + 1 :]], axis=2
        )
        arrived = with_halo(rim_rows, (("dev", 2),), 1)
        core_part = inner_part[:, :, 1 : local_rows + 1]
        core_part = core_part.at[:, :, :1].add(arrived[:, :, :1])
        core_part = core_part.at[:, :, local_rows - 1 :].add(arrived[:, :, 3:])
        returned = from_behind(core_part[:, :1], "group", -1)
        return core_part[:, 1:].at[:, local_planes - 1 :].add(returned)

    def apply_fsai(vector):
        return gather_lower(fsai_d, fsai_low, lower_window(vector), vector)

    def apply_fsai_transposed(vector):
        diagonal_part = block_mul_transposed(fsai_d, vector)
        upper_sum = push_upper(fsai_low, vector)
        return diagonal_part + upper_sum

    def residual_sum(weighted):
        return lax.psum(local_gram(weighted, weighted), ("group", "dev"))

    solution = jnp.zeros_like(right_side)
    residual = right_side
    weighted = apply_fsai(residual)
    resid_gram = residual_sum(weighted)
    direction = apply_fsai_transposed(weighted)
    for iteration in range(ITERS):
        lower_sum = gather_lower(stiff_d, stiff_low, lower_window(direction), direction)
        apply_upper_sum = push_upper(stiff_low, direction)
        product = lower_sum + apply_upper_sum
        step_size = gram_solve(
            lax.psum(local_gram(direction, product), ("group", "dev")), resid_gram
        )
        solution = solution + combine(direction, step_size)
        residual = residual - combine(product, step_size)
        if iteration + 1 < ITERS:
            weighted = apply_fsai(residual)
            next_gram = residual_sum(weighted)
            precond = apply_fsai_transposed(weighted)
            conjugacy = gram_solve(resid_gram, next_gram)
            direction = precond + combine(direction, conjugacy)
            resid_gram = next_gram
    return (solution, residual)


def solution(mesh):
    return jax.shard_map(
        per_device,
        mesh=mesh,
        in_specs=(
            P(None, "group", "dev", None, None),
            P(None, None, "group", "dev"),
            P(None, None, None, "group", "dev"),
            P(None, None, "group", "dev"),
            P(None, None, None, "group", "dev"),
            P(None, "group", "dev"),
        ),
        out_specs=(P(None, "group", "dev", None, None), P(None, "group", "dev", None, None)),
        check_vma=False,
    )
```

profile of v0, /device:TPU:1, one launch (start us, length us, event | category | flops | bytes accessed | tf_op | source)
XLA Modules:
  0.0 1071.7 jit_solution(4820610917557618189)
XLA Ops:
  8.3 4.5 collective-permute-start
  12.8 1.9 collective-permute-start.1
  25.8 3.7 collective-permute-start.2
  31.3 5.2 collective-permute-done.2
  37.8 1.2 multiply_add_fusion.290
  39.0 1.2 multiply_add_fusion.289
  40.2 1.2 multiply_add_fusion.288
  41.4 1.2 multiply_add_fusion.296
  42.6 1.2 multiply_add_fusion.295
  63.6 1.4 fusion.48
  65.1 4.8 collective-permute-start.3
  71.4 1.9 collective-permute-start.4
  74.1 5.4 collective-permute-done.4
  79.6 1.3 collective-permute-start.5
  81.5 1.4 convolution_bitcast_fusion.5
  83.0 3.7 collective-permute-done.5
  87.0 3.9 collective-permute-start.6
  90.9 2.1 collective-permute-start.7
  102.7 1.4 fusion.36
  104.2 3.6 collective-permute-start.9
  107.8 1.9 collective-permute-start.10
  109.8 3.9 collective-permute-start.8
  114.2 1.6 collective-permute-done.10
  116.0 1.3 collective-permute-start.11
  117.3 4.0 collective-permute-done.8
  126.9 1.4 convolution_bitcast_fusion.6
  128.6 264.0 %all-reduce.65.cloned.1.call-done = (f32[128,128]{0,1:T(8,128)}, f32[128,128]{0,1:T(8,128)}) async-done(((f32[128,128]{0,1:T(8,128)}, f32[128,128]{0,1:T(8,128)}), (f32[128,128]{0,1:T(8,128)}, f32[128,128]{0,1:T(8,128)})) %all-reduce.65.cloned.1.call-update) | async-done | bytes 131088 | tf_op jit(solution)/shard_map/psum | solution.py:139
  394.4 11.7 %cholesky.59 = f32[128,128]{1,0:T(8,128)S(1)} custom-call(f32[128,128]{1,0:T(8,128)S(1)} %fusion.164), custom_call_target="Cholesky" | custom-call | tf_op jit(solution)/shard_map/jit(cholesky)/cholesky | solution.py:67
  407.5 9.8 custom-call.13
  420.2 4.9 collective-permute-start.12
  425.1 1.9 collective-permute-start.13
  427.0 11.7 %cholesky.70 = f32[128,128]{1,0:T(8,128)S(1)} custom-call(f32[128,128]{1,0:T(8,128)S(1)} %fusion.160), custom_call_target="Cholesky" | custom-call | tf_op jit(solution)/shard_map/jit(cholesky)/cholesky | solution.py:67
  440.4 1.8 collective-permute-start.14
  444.2 6.4 collective-permute-done.14
  450.8 1.2 multiply_add_fusion.125
  453.0 1.2 multiply_add_fusion.124
  454.2 1.2 multiply_add_fusion.123
  455.4 1.2 multiply_add_fusion.128
  457.7 1.2 multiply_add_fusion.127
  458.9 1.2 multiply_add_fusion.126
  461.2 1.2 multiply_add_fusion.131
  477.7 1.4 fusion.24
  480.0 3.3 collective-permute-start.15
  483.9 10.4 custom-call.15
  494.3 1.9 collective-permute-start.16
  496.3 1.4 convolution_bitcast_fusion.3
  498.8 3.8 collective-permute-done.16
  503.7 1.3 collective-permute-start.17
  505.0 238.5 %all-reduce.61.cloned.1.call-done = f32[128,128]{1,0:T(8,128)} async-done(((f32[128,128]{1,0:T(8,128)}), f32[128,128]{1,0:T(8,128)}) %all-reduce.61.cloned.1.call-update) | async-done | bytes 65552 | tf_op jit(solution)/shard_map/psum | solution.py:139
  756.5 2.5 collective-permute-start.18
  759.0 1.9 collective-permute-start.19
  762.6 1.4 fusion.12
  764.1 4.4 collective-permute-start.21
  768.5 1.9 collective-permute-start.22
  770.5 2.7 collective-permute-start.20
  773.6 2.9 collective-permute-done.22
  776.7 1.5 collective-permute-start.23
  778.2 1.8 collective-permute-done.20
  785.8 1.4 convolution_bitcast_fusion.1
  787.2 249.6 %all-reduce.63.cloned.1.call-done = f32[128,128]{0,1:T(8,128)} async-done(((f32[128,128]{0,1:T(8,128)}), f32[128,128]{0,1:T(8,128)}) %all-reduce.63.cloned.1.call-update) | async-done | bytes 65552 | tf_op jit(solution)/shard_map/psum | solution.py:151
  1038.6 11.7 %cholesky.81 = f32[128,128]{1,0:T(8,128)S(1)} custom-call(f32[128,128]{1,0:T(8,128)S(1)} %fusion.156), custom_call_target="Cholesky" | custom-call | tf_op jit(solution)/shard_map/jit(cholesky)/cholesky | solution.py:67
  1051.7 9.8 custom-call.17
  1062.5 1.2 convolution_subtract_fusion
  1063.7 1.2 convolution_add_fusion
  (769 shorter events, 106.5 us)
Async XLA Ops:
  7.2 385.4 %all-reduce.65.cloned.1.call-start = ((), (), s32[]{:S(2)}) async-start(), calls=%async_computation.2 | async-start | bytes 262144 | tf_op jit(solution)/shard_map/psum | solution.py:139
  8.3 17.4 %collective-permute-start = (f32[3,2,1,64,128]{4,3,2,1,0:T(8,128)S(1)}, f32[3,2,1,64,128]{4,3,2,1,0:T(8,128)S(1)}, u32[]{:S(2)}, u32[]{:S(2)}) collective-permute-start(f32[3,2,1,64,128]{4,3,2,1,0:T(8,128)S(1)} %get-tuple-element.502), channel_id=1, source_target_pairs={{0,1},{1,2},{2,3},{3,4},{4,5},{5,6},{6,7},{7,8},{8,9},{9,10},{10,1... | collective-permute-start | bytes 589832 | tf_op jit(solution)/shard_map/ppermute | solution.py:18
  12.8 13.0 %collective-permute-start.1 = (f32[3,2,1,64,128]{4,3,2,1,0:T(8,128)S(1)}, f32[3,2,1,64,128]{4,3,2,1,0:T(8,128)S(1)}, u32[]{:S(2)}, u32[]{:S(2)}) collective-permute-start(f32[3,2,1,64,128]{4,3,2,1,0:T(8,128)S(1)} %get-tuple-element.501), channel_id=1, source_target_pairs={{1,0},{2,1},{3,2},{4,3},{5,4},{6,5},{7,6},{8,7},{9,8},{10,9},{11,1... | collective-permute-start | bytes 589832 | tf_op jit(solution)/shard_map/ppermute | solution.py:21
  18.4 102.9 %copy-start.17 = (f32[2,2,64]{2,1,0:T(2,128)}, f32[2,2,64]{2,1,0:T(2,128)S(1)}, u32[]{:S(2)}) copy-start(f32[2,2,64]{2,1,0:T(2,128)S(1)} %get-tuple-element.651) | copy-start | bytes 3076
  18.4 103.0 %copy-start.19 = (f32[2,2,64]{2,1,0:T(2,128)}, f32[2,2,64]{2,1,0:T(2,128)S(1)}, u32[]{:S(2)}) copy-start(f32[2,2,64]{2,1,0:T(2,128)S(1)} %get-tuple-element.658) | copy-start | bytes 3076
  18.4 103.0 %copy-start.21 = (f32[2,2,64]{2,1,0:T(2,128)}, f32[2,2,64]{2,1,0:T(2,128)S(1)}, u32[]{:S(2)}) copy-start(f32[2,2,64]{2,1,0:T(2,128)S(1)} %get-tuple-element.659) | copy-start | bytes 3076
  18.4 103.4 %copy-start.11 = (f32[2,2,64]{2,1,0:T(2,128)}, f32[2,2,64]{2,1,0:T(2,128)S(1)}, u32[]{:S(2)}) copy-start(f32[2,2,64]{2,1,0:T(2,128)S(1)} %get-tuple-element.655) | copy-start | bytes 3076
  18.4 103.4 %copy-start.13 = (f32[2,2,64]{2,1,0:T(2,128)}, f32[2,2,64]{2,1,0:T(2,128)S(1)}, u32[]{:S(2)}) copy-start(f32[2,2,64]{2,1,0:T(2,128)S(1)} %get-tuple-element.656) | copy-start | bytes 3076
  18.5 103.4 %copy-start.15 = (f32[2,2,64]{2,1,0:T(2,128)}, f32[2,2,64]{2,1,0:T(2,128)S(1)}, u32[]{:S(2)}) copy-start(f32[2,2,64]{2,1,0:T(2,128)S(1)} %get-tuple-element.657) | copy-start | bytes 3076
  18.5 104.0 %copy-start.5 = (f32[2,2,64]{2,1,0:T(2,128)}, f32[2,2,64]{2,1,0:T(2,128)S(1)}, u32[]{:S(2)}) copy-start(f32[2,2,64]{2,1,0:T(2,128)S(1)} %get-tuple-element.652) | copy-start | bytes 3076
  18.5 104.0 %copy-start.7 = (f32[2,2,64]{2,1,0:T(2,128)}, f32[2,2,64]{2,1,0:T(2,128)S(1)}, u32[]{:S(2)}) copy-start(f32[2,2,64]{2,1,0:T(2,128)S(1)} %get-tuple-element.653) | copy-start | bytes 3076
  18.5 104.0 %copy-start.9 = (f32[2,2,64]{2,1,0:T(2,128)}, f32[2,2,64]{2,1,0:T(2,128)S(1)}, u32[]{:S(2)}) copy-start(f32[2,2,64]{2,1,0:T(2,128)S(1)} %get-tuple-element.654) | copy-start | bytes 3076
  19.2 42.9 %copy-start.130 = (f32[2,2,64]{2,1,0:T(2,128)}, f32[2,2,64]{2,1,0:T(2,128)S(1)}, u32[]{:S(2)}) copy-start(f32[2,2,64]{2,1,0:T(2,128)S(1)} %get-tuple-element.897) | copy-start | bytes 3076
  19.2 44.0 %copy-start.119 = (f32[2,2,64]{2,1,0:T(2,128)}, f32[2,2,64]{2,1,0:T(2,128)S(1)}, u32[]{:S(2)}) copy-start(f32[2,2,64]{2,1,0:T(2,128)S(1)} %get-tuple-element.896) | copy-start | bytes 3076
  19.2 44.0 %copy-start.122 = (f32[2,2,64]{2,1,0:T(2,128)}, f32[2,2,64]{2,1,0:T(2,128)S(1)}, u32[]{:S(2)}) copy-start(f32[2,2,64]{2,1,0:T(2,128)S(1)} %get-tuple-element.899) | copy-start | bytes 3076
  19.2 44.0 %copy-start.125 = (f32[2,2,64]{2,1,0:T(2,128)}, f32[2,2,64]{2,1,0:T(2,128)S(1)}, u32[]{:S(2)}) copy-start(f32[2,2,64]{2,1,0:T(2,128)S(1)} %get-tuple-element.902) | copy-start | bytes 3076
  19.8 43.4 %copy-start.134 = (f32[2,2,64]{2,1,0:T(2,128)}, f32[2,2,64]{2,1,0:T(2,128)S(1)}, u32[]{:S(2)}) copy-start(f32[2,2,64]{2,1,0:T(2,128)S(1)} %get-tuple-element.831) | copy-start | bytes 3076
  19.8 43.4 %copy-start.136 = (f32[2,2,64]{2,1,0:T(2,128)}, f32[2,2,64]{2,1,0:T(2,128)S(1)}, u32[]{:S(2)}) copy-start(f32[2,2,64]{2,1,0:T(2,128)S(1)} %get-tuple-element.833) | copy-start | bytes 3076
  19.8 43.4 %copy-start.138 = (f32[2,2,64]{2,1,0:T(2,128)}, f32[2,2,64]{2,1,0:T(2,128)S(1)}, u32[]{:S(2)}) copy-start(f32[2,2,64]{2,1,0:T(2,128)S(1)} %get-tuple-element.834) | copy-start | bytes 3076
  19.9 43.4 %copy-start.140 = (f32[2,2,64]{2,1,0:T(2,128)}, f32[2,2,64]{2,1,0:T(2,128)S(1)}, u32[]{:S(2)}) copy-start(f32[2,2,64]{2,1,0:T(2,128)S(1)} %get-tuple-element.836) | copy-start | bytes 3076
  19.9 43.4 %copy-start.142 = (f32[2,2,64]{2,1,0:T(2,128)}, f32[2,2,64]{2,1,0:T(2,128)S(1)}, u32[]{:S(2)}) copy-start(f32[2,2,64]{2,1,0:T(2,128)S(1)} %get-tuple-element.837) | copy-start | bytes 3076
  19.9 43.4 %copy-start.144 = (f32[2,2,64]{2,1,0:T(2,128)}, f32[2,2,64]{2,1,0:T(2,128)S(1)}, u32[]{:S(2)}) copy-start(f32[2,2,64]{2,1,0:T(2,128)S(1)} %get-tuple-element.839) | copy-start | bytes 3076
  23.2 101.7 %copy-start.47 = (f32[2,2,64]{2,1,0:T(2,128)}, f32[2,2,64]{2,1,0:T(2,128)S(1)}, u32[]{:S(2)}) copy-start(f32[2,2,64]{2,1,0:T(2,128)S(1)} %get-tuple-element.634) | copy-start | bytes 3076
  23.2 101.7 %copy-start.49 = (f32[2,2,64]{2,1,0:T(2,128)}, f32[2,2,64]{2,1,0:T(2,128)S(1)}, u32[]{:S(2)}) copy-start(f32[2,2,64]{2,1,0:T(2,128)S(1)} %get-tuple-element.635) | copy-start | bytes 3076
  23.2 101.7 %copy-start.51 = (f32[2,2,64]{2,1,0:T(2,128)}, f32[2,2,64]{2,1,0:T(2,128)S(1)}, u32[]{:S(2)}) copy-start(f32[2,2,64]{2,1,0:T(2,128)S(1)} %get-tuple-element.636) | copy-start | bytes 3076
  23.2 102.1 %copy-start.23 = (f32[2,2,64]{2,1,0:T(2,128)}, f32[2,2,64]{2,1,0:T(2,128)S(1)}, u32[]{:S(2)}) copy-start(f32[2,2,64]{2,1,0:T(2,128)S(1)} %get-tuple-element.633) | copy-start | bytes 3076
  23.2 102.1 %copy-start.25 = (f32[2,2,64]{2,1,0:T(2,128)}, f32[2,2,64]{2,1,0:T(2,128)S(1)}, u32[]{:S(2)}) copy-start(f32[2,2,64]{2,1,0:T(2,128)S(1)} %get-tuple-element.637) | copy-start | bytes 3076
  23.2 102.1 %copy-start.27 = (f32[2,2,64]{2,1,0:T(2,128)}, f32[2,2,64]{2,1,0:T(2,128)S(1)}, u32[]{:S(2)}) copy-start(f32[2,2,64]{2,1,0:T(2,128)S(1)} %get-tuple-element.638) | copy-start | bytes 3076
  23.2 102.1 %copy-start.29 = (f32[2,2,64]{2,1,0:T(2,128)}, f32[2,2,64]{2,1,0:T(2,128)S(1)}, u32[]{:S(2)}) copy-start(f32[2,2,64]{2,1,0:T(2,128)S(1)} %get-tuple-element.639) | copy-start | bytes 3076
  23.2 102.1 %copy-start.31 = (f32[2,2,64]{2,1,0:T(2,128)}, f32[2,2,64]{2,1,0:T(2,128)S(1)}, u32[]{:S(2)}) copy-start(f32[2,2,64]{2,1,0:T(2,128)S(1)} %get-tuple-element.640) | copy-start | bytes 3076
  23.2 102.1 %copy-start.33 = (f32[2,2,64]{2,1,0:T(2,128)}, f32[2,2,64]{2,1,0:T(2,128)S(1)}, u32[]{:S(2)}) copy-start(f32[2,2,64]{2,1,0:T(2,128)S(1)} %get-tuple-element.641) | copy-start | bytes 3076
  23.2 102.1 %copy-start.35 = (f32[2,2,64]{2,1,0:T(2,128)}, f32[2,2,64]{2,1,0:T(2,128)S(1)}, u32[]{:S(2)}) copy-start(f32[2,2,64]{2,1,0:T(2,128)S(1)} %get-tuple-element.851) | copy-start | bytes 3076
  23.2 102.1 %copy-start.37 = (f32[2,2,64]{2,1,0:T(2,128)}, f32[2,2,64]{2,1,0:T(2,128)S(1)}, u32[]{:S(2)}) copy-start(f32[2,2,64]{2,1,0:T(2,128)S(1)} %get-tuple-element.852) | copy-start | bytes 3076
  23.2 102.1 %copy-start.39 = (f32[2,2,64]{2,1,0:T(2,128)}, f32[2,2,64]{2,1,0:T(2,128)S(1)}, u32[]{:S(2)}) copy-start(f32[2,2,64]{2,1,0:T(2,128)S(1)} %get-tuple-element.853) | copy-start | bytes 3076
  23.2 102.1 %copy-start.41 = (f32[2,2,64]{2,1,0:T(2,128)}, f32[2,2,64]{2,1,0:T(2,128)S(1)}, u32[]{:S(2)}) copy-start(f32[2,2,64]{2,1,0:T(2,128)S(1)} %get-tuple-element.854) | copy-start | bytes 3076
  23.3 102.1 %copy-start.43 = (f32[2,2,64]{2,1,0:T(2,128)}, f32[2,2,64]{2,1,0:T(2,128)S(1)}, u32[]{:S(2)}) copy-start(f32[2,2,64]{2,1,0:T(2,128)S(1)} %get-tuple-element.855) | copy-start | bytes 3076
  23.3 102.1 %copy-start.45 = (f32[2,2,64]{2,1,0:T(2,128)}, f32[2,2,64]{2,1,0:T(2,128)S(1)}, u32[]{:S(2)}) copy-start(f32[2,2,64]{2,1,0:T(2,128)S(1)} %get-tuple-element.856) | copy-start | bytes 3076
  23.9 101.0 %copy-start.53 = (f32[2,2,64]{2,1,0:T(2,128)}, f32[2,2,64]{2,1,0:T(2,128)S(1)}, u32[]{:S(2)}) copy-start(f32[2,2,64]{2,1,0:T(2,128)S(1)} %get-tuple-element.615) | copy-start | bytes 3076
  25.8 10.7 collective-permute-start.2
  65.1 8.9 collective-permute-start.3
  71.4 8.0 collective-permute-start.4
  79.6 7.2 collective-permute-start.5
  87.0 14.7 %collective-permute-start.6 = (f32[3,2,1,64,128]{4,3,2,1,0:T(8,128)S(1)}, f32[3,2,1,64,128]{4,3,2,1,0:T(8,128)S(1)}, u32[]{:S(2)}, u32[]{:S(2)}) collective-permute-start(f32[3,2,1,64,128]{4,3,2,1,0:T(8,128)S(1)} %get-tuple-element.416), channel_id=1, source_target_pairs={{0,1},{1,2},{2,3},{3,4},{4,5},{5,6},{6,7},{7,8},{8,9},{9,10},{10,1... | collective-permute-start | bytes 589832 | tf_op jit(solution)/shard_map/ppermute | solution.py:18
  90.9 18.8 %collective-permute-start.7 = (f32[3,2,1,64,128]{4,3,2,1,0:T(8,128)S(1)}, f32[3,2,1,64,128]{4,3,2,1,0:T(8,128)S(1)}, u32[]{:S(2)}, u32[]{:S(2)}) collective-permute-start(f32[3,2,1,64,128]{4,3,2,1,0:T(8,128)S(1)} %get-tuple-element.417), channel_id=1, source_target_pairs={{1,0},{2,1},{3,2},{4,3},{5,4},{6,5},{7,6},{8,7},{9,8},{10,9},{11,1... | collective-permute-start | bytes 589832 | tf_op jit(solution)/shard_map/ppermute | solution.py:21
  104.2 10.0 collective-permute-start.9
  107.8 8.0 collective-permute-start.10
  109.8 11.5 %collective-permute-start.8 = (f32[3,1,4,64,128]{4,3,2,1,0:T(8,128)S(1)}, f32[3,1,4,64,128]{4,3,2,1,0:T(8,128)S(1)}, u32[]{:S(2)}, u32[]{:S(2)}) collective-permute-start(f32[3,1,4,64,128]{4,3,2,1,0:T(8,128)S(1)} %pad_maximum_fusion.5), channel_id=1, source_target_pairs={{0,32},{32,64},{64,96},{96,128},{128,160},{160,192},{192,224},{1,3... | collective-permute-start | bytes 1179656 | tf_op jit(solution)/shard_map/ppermute | solution.py:29
  116.0 10.2 collective-permute-start.11
  128.4 615.1 %all-reduce.61.cloned.1.call-start = ((), (), s32[]{:S(2)}) async-start(), calls=%async_computation | async-start | bytes 131072 | tf_op jit(solution)/shard_map/psum | solution.py:139
  420.2 20.2 %collective-permute-start.12 = (f32[3,2,1,64,128]{4,3,2,1,0:T(8,128)S(1)}, f32[3,2,1,64,128]{4,3,2,1,0:T(8,128)S(1)}, u32[]{:S(2)}, u32[]{:S(2)}) collective-permute-start(f32[3,2,1,64,128]{4,3,2,1,0:T(8,128)S(1)} %get-tuple-element.410), channel_id=1, source_target_pairs={{0,1},{1,2},{2,3},{3,4},{4,5},{5,6},{6,7},{7,8},{8,9},{9,10},{10,1... | collective-permute-start | bytes 589832 | tf_op jit(solution)/shard_map/ppermute | solution.py:18
  425.1 15.3 %collective-permute-start.13 = (f32[3,2,1,64,128]{4,3,2,1,0:T(8,128)S(1)}, f32[3,2,1,64,128]{4,3,2,1,0:T(8,128)S(1)}, u32[]{:S(2)}, u32[]{:S(2)}) collective-permute-start(f32[3,2,1,64,128]{4,3,2,1,0:T(8,128)S(1)} %get-tuple-element.411), channel_id=1, source_target_pairs={{1,0},{2,1},{3,2},{4,3},{5,4},{6,5},{7,6},{8,7},{9,8},{10,9},{11,1... | collective-permute-start | bytes 589832 | tf_op jit(solution)/shard_map/ppermute | solution.py:21
  440.4 10.2 collective-permute-start.14
  480.0 17.8 %collective-permute-start.15 = (f32[3,3,1,64,128]{4,3,2,1,0:T(8,128)}, f32[3,3,1,64,128]{4,3,2,1,0:T(8,128)}, u32[]{:S(2)}, u32[]{:S(2)}) collective-permute-start(f32[3,3,1,64,128]{4,3,2,1,0:T(8,128)} %get-tuple-element.166), channel_id=1, source_target_pairs={{0,1},{1,2},{2,3},{3,4},{4,5},{5,6},{6,7},{7,8},{8,9},{9,10},{10,1... | collective-permute-start | bytes 884744 | tf_op jit(solution)/shard_map/ppermute | solution.py:18
  494.3 8.3 collective-permute-start.16
  497.7 245.8 %copy-start.3 = (f32[1,128,128]{1,2,0:T(8,128)S(1)}, f32[1,128,128]{1,2,0:T(8,128)}, u32[]{:S(2)}) copy-start(f32[1,128,128]{1,2,0:T(8,128)} %custom-call.15) | copy-start | bytes 196612
  497.8 539.1 %all-reduce.63.cloned.1.call-start = ((), (), s32[]{:S(2)}) async-start(), calls=%async_computation.1 | async-start | bytes 131072 | tf_op jit(solution)/shard_map/psum | solution.py:151
  503.7 241.2 %collective-permute-start.17 = (f32[3,1,2,64,128]{4,3,2,1,0:T(8,128)S(1)}, f32[3,1,2,64,128]{4,3,2,1,0:T(8,128)S(1)}, u32[]{:S(2)}, u32[]{:S(2)}) collective-permute-start(f32[3,1,2,64,128]{4,3,2,1,0:T(8,128)S(1)} %slice.4621), channel_id=1, source_target_pairs={{32,0},{64,32},{96,64},{128,96},{160,128},{192,160},{224,192},{33,... | collective-permute-start | bytes 589832 | tf_op jit(solution)/shard_map/ppermute | solution.py:29
  756.5 5.1 collective-permute-start.18
  759.0 11.4 %collective-permute-start.19 = (f32[3,2,1,64,128]{4,3,2,1,0:T(8,128)S(1)}, f32[3,2,1,64,128]{4,3,2,1,0:T(8,128)S(1)}, u32[]{:S(2)}, u32[]{:S(2)}) collective-permute-start(f32[3,2,1,64,128]{4,3,2,1,0:T(8,128)S(1)} %get-tuple-element.325), channel_id=1, source_target_pairs={{1,0},{2,1},{3,2},{4,3},{5,4},{6,5},{7,6},{8,7},{9,8},{10,9},{11,1... | collective-permute-start | bytes 589832 | tf_op jit(solution)/shard_map/ppermute | solution.py:21
  764.1 9.5 collective-permute-start.21
  768.5 8.0 collective-permute-start.22
  770.5 9.5 collective-permute-start.20
  776.7 8.3 collective-permute-start.23
  785.8 275.7 %copy-start.2 = (f32[128,128]{1,0:T(8,128)S(1)}, f32[128,128]{1,0:T(8,128)}, u32[]{:S(2)}) copy-start(f32[128,128]{1,0:T(8,128)} %all-reduce.61.cloned.1.call-done) | copy-start | bytes 196612
  (243 other events, 1343.4 us)
Sparse Core Ops, SparseCore 0:
  128.5 264.0 all-reduce.64
  497.9 245.5 all-reduce.60
  787.4 249.4 all-reduce.62
where the time goes:
time: 1080 us; the launch traced here: 1070 us
  waiting for transfers between devices  788 us (73%)
  other arithmetic  168 us (16%)
  starting transfers between devices  65.3 us (6%)
  between operations  19.7 us (2%)
  local copies, waits for them, and re-layouts  17.9 us (2%)
  matrix products  12.7 us (1%)
    psum x2, waiting for transfers between devices, residual_sum(): return lax.psum(local_gram(weighted, weighted), ('group', 'dev'))  502 us
    psum x1, waiting for transfers between devices, per_device(): lax.psum(local_gram(direction, product), ('group', 'dev'))  250 us
    add x55, other arithmetic, block_mul(): coeffs[target, 0][..., None] * vector[0]  42.9 us
    add x50, other arithmetic, block_mul_transposed(): coeffs[0, target][..., None] * vector[0]  41.6 us
    another operation x9, other arithmetic, gram_solve(): factor = jnp.linalg.cholesky(matrix)  37.2 us
    ppermute x8, starting transfers between devices, with_halo(): lax.ppermute(lax.slice_in_dim(block, block.shape[dim] - width, None, axis...  32 us
    another operation x6, other arithmetic, gram_solve(): lax.linalg.triangular_solve(factor, halfway, left_side=True, lower=True,...  32 us
  transfers between devices with their start and end apart: 27, of which 13 were waited for; matrix products, arithmetic and copies ran while one was open for 7% of the time, Pallas kernels for 0%

commit v1 on v0

--- a/solution.py
+++ b/solution.py
@@ -148,7 +148,7 @@
         apply_upper_sum = push_upper(stiff_low, direction)
         product = lower_sum + apply_upper_sum
         step_size = gram_solve(
-            lax.psum(local_gram(direction, product), ("group", "dev")), resid_gram
+            lax.psum(lax.psum(local_gram(direction, product), "dev"), "group"), resid_gram
         )
         solution = solution + combine(direction, step_size)
         residual = residual - combine(product, step_size)

time: 1080 us -> 1480 us (1.37)
  waiting for transfers between devices: 788 us -> 1180 us
    psum x1 -> x4, waiting for transfers between devices: 250 us -> 668 us  [the longest x2 517 us: per_device(): lax.psum(local_gram(direction, product), 'dev')]
  transfers between devices with their start and end apart: 27 -> 30, of which waited for: 13 -> 16; matrix products, arithmetic and copies ran while one was open for 7% -> 5% of each run, Pallas kernels for 0% -> 0%
where the time goes in v1:
time: 1480 us; the launch traced here: 1470 us
  waiting for transfers between devices  1180 us (80%)
  other arithmetic  167 us (11%)
  starting transfers between devices  69.8 us (5%)
  between operations  22.1 us (1%)
  local copies, waits for them, and re-layouts  18.3 us (1%)
    psum x2, waiting for transfers between devices, per_device(): lax.psum(local_gram(direction, product), 'dev')  517 us
    psum x2, waiting for transfers between devices, residual_sum(): return lax.psum(local_gram(weighted, weighted), ('group', 'dev'))  490 us
    psum x2, waiting for transfers between devices, per_device(): lax.psum(lax.psum(local_gram(direction, product), 'dev'), 'group')  150 us
    add x50, other arithmetic, block_mul_transposed(): coeffs[0, target][..., None] * vector[0]  41.6 us
    add x55, other arithmetic, block_mul(): coeffs[target, 0][..., None] * vector[0]  40.3 us
    another operation x9, other arithmetic, gram_solve(): factor = jnp.linalg.cholesky(matrix)  37.2 us
    ppermute x8, starting transfers between devices, with_halo(): lax.ppermute(lax.slice_in_dim(block, block.shape[dim] - width, None, axis...  35.7 us
    another operation x6, other arithmetic, gram_solve(): lax.linalg.triangular_solve(factor, halfway, left_side=True, lower=True,...  32 us
  transfers between devices with their start and end apart: 30, of which 16 were waited for; matrix products, arithmetic and copies ran while one was open for 5% of the time, Pallas kernels for 0%

profile of v1, /device:TPU:1, one launch (start us, length us, event | category | flops | bytes accessed | tf_op | source)
XLA Modules:
  0.0 1473.6 jit_solution(999267388205070625)
XLA Ops:
  9.1 4.5 collective-permute-start
  13.6 1.9 collective-permute-start.1
  27.4 3.7 collective-permute-start.2
  32.9 5.2 collective-permute-done.2
  40.5 1.2 multiply_add_fusion.289
  41.7 1.2 multiply_add_fusion.288
  42.9 1.2 multiply_add_fusion.296
  44.1 1.2 multiply_add_fusion.295
  45.4 1.2 multiply_add_fusion.294
  65.3 1.4 fusion.48
  67.6 4.8 collective-permute-start.3
  72.5 1.9 collective-permute-start.4
  74.4 1.4 convolution_bitcast_fusion.5
  76.6 247.9 %all-reduce.67.cloned.1.call-done = f32[128,128]{0,1:T(8,128)} async-done(((f32[128,128]{0,1:T(8,128)}), f32[128,128]{0,1:T(8,128)}) %all-reduce.67.cloned.1.call-update) | async-done | bytes 65552 | tf_op jit(solution)/shard_map/psum | solution.py:139
  326.6 1.5 collective-permute-start.5
  328.1 11.7 cholesky.70
  340.2 2.5 collective-permute-start.6
  342.6 1.9 collective-permute-start.7
  353.8 1.4 fusion.36
  355.3 3.6 collective-permute-start.9
  359.0 1.9 collective-permute-start.10
  360.9 4.3 collective-permute-start.8
  365.6 1.4 collective-permute-done.10
  367.1 1.5 collective-permute-start.11
  368.7 4.1 collective-permute-done.8
  378.4 1.4 convolution_bitcast_fusion.6
  379.9 257.8 %all-reduce.63.cloned.1.call-done = f32[128,128]{0,1:T(8,128)} async-done(((f32[128,128]{0,1:T(8,128)}), f32[128,128]{0,1:T(8,128)}) %all-reduce.63.cloned.1.call-update) | async-done | bytes 65552 | tf_op jit(solution)/shard_map/psum | solution.py:151
  638.5 74.7 %all-reduce.65.cloned.1.call-done = f32[128,128]{0,1:T(8,128)} async-done(((f32[128,128]{0,1:T(8,128)}), f32[128,128]{0,1:T(8,128)}) %all-reduce.65.cloned.1.call-update) | async-done | bytes 65552 | tf_op jit(solution)/shard_map/psum | solution.py:151
  715.0 11.7 cholesky.59
  728.1 9.8 custom-call.13
  739.0 8.6 collective-permute-start.12
  747.5 1.9 collective-permute-start.13
  750.1 4.4 collective-permute-done.13
  754.5 1.7 collective-permute-start.14
  758.3 3.0 collective-permute-done.14
  763.7 1.2 multiply_add_fusion.124
  766.1 1.2 multiply_add_fusion.128
  768.4 1.2 multiply_add_fusion.127
  769.6 1.2 multiply_add_fusion.126
  772.0 1.2 multiply_add_fusion.131
  788.4 1.4 fusion.24
  790.7 4.9 collective-permute-start.15
  796.3 10.4 custom-call.15
  806.7 1.9 collective-permute-start.16
  808.6 1.4 convolution_bitcast_fusion.3
  811.2 3.8 collective-permute-done.16
  816.1 1.3 collective-permute-start.17
  817.4 241.7 %all-reduce.69.cloned.1.call-done = f32[128,128]{1,0:T(8,128)} async-done(((f32[128,128]{1,0:T(8,128)}), f32[128,128]{1,0:T(8,128)}) %all-reduce.69.cloned.1.call-update) | async-done | bytes 65552 | tf_op jit(solution)/shard_map/psum | solution.py:139
  1072.1 2.5 collective-permute-start.18
  1074.6 1.9 collective-permute-start.19
  1077.6 1.4 fusion.12
  1079.1 4.4 collective-permute-start.21
  1083.5 1.9 collective-permute-start.22
  1085.5 2.7 collective-permute-start.20
  1088.6 2.9 collective-permute-done.22
  1091.7 1.5 collective-permute-start.23
  1093.2 1.8 collective-permute-done.20
  1100.7 1.4 convolution_bitcast_fusion.1
  1102.5 259.6 %all-reduce.71.cloned.1.call-done = f32[128,128]{0,1:T(8,128)} async-done(((f32[128,128]{0,1:T(8,128)}), f32[128,128]{0,1:T(8,128)}) %all-reduce.71.cloned.1.call-update) | async-done | bytes 65552 | tf_op jit(solution)/shard_map/psum | solution.py:151
  1362.1 75.6 %all-reduce.73.cloned.1.call-done = f32[128,128]{0,1:T(8,128)} async-done(((f32[128,128]{0,1:T(8,128)}), f32[128,128]{0,1:T(8,128)}) %all-reduce.73.cloned.1.call-update) | async-done | bytes 65552 | tf_op jit(solution)/shard_map/psum | solution.py:151
  1439.5 11.7 cholesky.81
  1452.5 9.8 custom-call.17
  1463.3 1.2 convolution_subtract_fusion
  1464.6 1.2 convolution_add_fusion
  (808 shorter events, 107.3 us)
Async XLA Ops:
  8.0 316.4 %all-reduce.67.cloned.1.call-start = ((), (), s32[]{:S(2)}) async-start(), calls=%async_computation.2 | async-start | bytes 131072 | tf_op jit(solution)/shard_map/psum | solution.py:139
  9.1 18.1 %collective-permute-start = (f32[3,2,1,64,128]{4,3,2,1,0:T(8,128)S(1)}, f32[3,2,1,64,128]{4,3,2,1,0:T(8,128)S(1)}, u32[]{:S(2)}, u32[]{:S(2)}) collective-permute-start(f32[3,2,1,64,128]{4,3,2,1,0:T(8,128)S(1)} %get-tuple-element.500), channel_id=1, source_target_pairs={{0,1},{1,2},{2,3},{3,4},{4,5},{5,6},{6,7},{7,8},{8,9},{9,10},{10,1... | collective-permute-start | bytes 589832 | tf_op jit(solution)/shard_map/ppermute | solution.py:18
  13.6 13.7 collective-permute-start.1
  19.3 353.5 %copy-start.19 = (f32[2,2,64]{2,1,0:T(2,128)}, f32[2,2,64]{2,1,0:T(2,128)S(1)}, u32[]{:S(2)}) copy-start(f32[2,2,64]{2,1,0:T(2,128)S(1)} %get-tuple-element.649) | copy-start | bytes 3076
  19.3 353.5 %copy-start.21 = (f32[2,2,64]{2,1,0:T(2,128)}, f32[2,2,64]{2,1,0:T(2,128)S(1)}, u32[]{:S(2)}) copy-start(f32[2,2,64]{2,1,0:T(2,128)S(1)} %get-tuple-element.656) | copy-start | bytes 3076
  19.3 353.5 %copy-start.23 = (f32[2,2,64]{2,1,0:T(2,128)}, f32[2,2,64]{2,1,0:T(2,128)S(1)}, u32[]{:S(2)}) copy-start(f32[2,2,64]{2,1,0:T(2,128)S(1)} %get-tuple-element.657) | copy-start | bytes 3076
  19.3 354.0 %copy-start.13 = (f32[2,2,64]{2,1,0:T(2,128)}, f32[2,2,64]{2,1,0:T(2,128)S(1)}, u32[]{:S(2)}) copy-start(f32[2,2,64]{2,1,0:T(2,128)S(1)} %get-tuple-element.653) | copy-start | bytes 3076
  19.4 354.0 %copy-start.15 = (f32[2,2,64]{2,1,0:T(2,128)}, f32[2,2,64]{2,1,0:T(2,128)S(1)}, u32[]{:S(2)}) copy-start(f32[2,2,64]{2,1,0:T(2,128)S(1)} %get-tuple-element.654) | copy-start | bytes 3076
  19.4 354.0 %copy-start.17 = (f32[2,2,64]{2,1,0:T(2,128)}, f32[2,2,64]{2,1,0:T(2,128)S(1)}, u32[]{:S(2)}) copy-start(f32[2,2,64]{2,1,0:T(2,128)S(1)} %get-tuple-element.655) | copy-start | bytes 3076
  19.4 354.6 %copy-start.7 = (f32[2,2,64]{2,1,0:T(2,128)}, f32[2,2,64]{2,1,0:T(2,128)S(1)}, u32[]{:S(2)}) copy-start(f32[2,2,64]{2,1,0:T(2,128)S(1)} %get-tuple-element.650) | copy-start | bytes 3076
  19.4 354.6 %copy-start.9 = (f32[2,2,64]{2,1,0:T(2,128)}, f32[2,2,64]{2,1,0:T(2,128)S(1)}, u32[]{:S(2)}) copy-start(f32[2,2,64]{2,1,0:T(2,128)S(1)} %get-tuple-element.651) | copy-start | bytes 3076
  19.4 354.6 %copy-start.11 = (f32[2,2,64]{2,1,0:T(2,128)}, f32[2,2,64]{2,1,0:T(2,128)S(1)}, u32[]{:S(2)}) copy-start(f32[2,2,64]{2,1,0:T(2,128)S(1)} %get-tuple-element.652) | copy-start | bytes 3076
  20.1 43.7 %copy-start.157 = (f32[2,2,64]{2,1,0:T(2,128)}, f32[2,2,64]{2,1,0:T(2,128)S(1)}, u32[]{:S(2)}) copy-start(f32[2,2,64]{2,1,0:T(2,128)S(1)} %get-tuple-element.892) | copy-start | bytes 3076
  20.1 43.7 %copy-start.159 = (f32[2,2,64]{2,1,0:T(2,128)}, f32[2,2,64]{2,1,0:T(2,128)S(1)}, u32[]{:S(2)}) copy-start(f32[2,2,64]{2,1,0:T(2,128)S(1)} %get-tuple-element.895) | copy-start | bytes 3076
  20.1 43.7 %copy-start.161 = (f32[2,2,64]{2,1,0:T(2,128)}, f32[2,2,64]{2,1,0:T(2,128)S(1)}, u32[]{:S(2)}) copy-start(f32[2,2,64]{2,1,0:T(2,128)S(1)} %get-tuple-element.898) | copy-start | bytes 3076
  20.1 44.8 %copy-start.151 = (f32[2,2,64]{2,1,0:T(2,128)}, f32[2,2,64]{2,1,0:T(2,128)S(1)}, u32[]{:S(2)}) copy-start(f32[2,2,64]{2,1,0:T(2,128)S(1)} %get-tuple-element.894) | copy-start | bytes 3076
  20.1 44.8 %copy-start.153 = (f32[2,2,64]{2,1,0:T(2,128)}, f32[2,2,64]{2,1,0:T(2,128)S(1)}, u32[]{:S(2)}) copy-start(f32[2,2,64]{2,1,0:T(2,128)S(1)} %get-tuple-element.897) | copy-start | bytes 3076
  20.1 44.8 %copy-start.155 = (f32[2,2,64]{2,1,0:T(2,128)}, f32[2,2,64]{2,1,0:T(2,128)S(1)}, u32[]{:S(2)}) copy-start(f32[2,2,64]{2,1,0:T(2,128)S(1)} %get-tuple-element.900) | copy-start | bytes 3076
  20.8 43.0 %copy-start.187 = (f32[2,2,64]{2,1,0:T(2,128)}, f32[2,2,64]{2,1,0:T(2,128)S(1)}, u32[]{:S(2)}) copy-start(f32[2,2,64]{2,1,0:T(2,128)S(1)} %get-tuple-element.830) | copy-start | bytes 3076
  20.8 44.1 %copy-start.163 = (f32[2,2,64]{2,1,0:T(2,128)}, f32[2,2,64]{2,1,0:T(2,128)S(1)}, u32[]{:S(2)}) copy-start(f32[2,2,64]{2,1,0:T(2,128)S(1)} %get-tuple-element.829) | copy-start | bytes 3076
  20.8 44.1 %copy-start.165 = (f32[2,2,64]{2,1,0:T(2,128)}, f32[2,2,64]{2,1,0:T(2,128)S(1)}, u32[]{:S(2)}) copy-start(f32[2,2,64]{2,1,0:T(2,128)S(1)} %get-tuple-element.831) | copy-start | bytes 3076
  20.8 44.1 %copy-start.167 = (f32[2,2,64]{2,1,0:T(2,128)}, f32[2,2,64]{2,1,0:T(2,128)S(1)}, u32[]{:S(2)}) copy-start(f32[2,2,64]{2,1,0:T(2,128)S(1)} %get-tuple-element.832) | copy-start | bytes 3076
  20.8 44.1 %copy-start.169 = (f32[2,2,64]{2,1,0:T(2,128)}, f32[2,2,64]{2,1,0:T(2,128)S(1)}, u32[]{:S(2)}) copy-start(f32[2,2,64]{2,1,0:T(2,128)S(1)} %get-tuple-element.834) | copy-start | bytes 3076
  20.8 44.1 %copy-start.171 = (f32[2,2,64]{2,1,0:T(2,128)}, f32[2,2,64]{2,1,0:T(2,128)S(1)}, u32[]{:S(2)}) copy-start(f32[2,2,64]{2,1,0:T(2,128)S(1)} %get-tuple-element.835) | copy-start | bytes 3076
  20.8 44.1 %copy-start.173 = (f32[2,2,64]{2,1,0:T(2,128)}, f32[2,2,64]{2,1,0:T(2,128)S(1)}, u32[]{:S(2)}) copy-start(f32[2,2,64]{2,1,0:T(2,128)S(1)} %get-tuple-element.837) | copy-start | bytes 3076
  24.1 352.7 %copy-start.25 = (f32[2,2,64]{2,1,0:T(2,128)}, f32[2,2,64]{2,1,0:T(2,128)S(1)}, u32[]{:S(2)}) copy-start(f32[2,2,64]{2,1,0:T(2,128)S(1)} %get-tuple-element.631) | copy-start | bytes 3076
  24.1 352.7 %copy-start.27 = (f32[2,2,64]{2,1,0:T(2,128)}, f32[2,2,64]{2,1,0:T(2,128)S(1)}, u32[]{:S(2)}) copy-start(f32[2,2,64]{2,1,0:T(2,128)S(1)} %get-tuple-element.635) | copy-start | bytes 3076
  24.1 352.7 %copy-start.29 = (f32[2,2,64]{2,1,0:T(2,128)}, f32[2,2,64]{2,1,0:T(2,128)S(1)}, u32[]{:S(2)}) copy-start(f32[2,2,64]{2,1,0:T(2,128)S(1)} %get-tuple-element.636) | copy-start | bytes 3076
  24.1 352.7 %copy-start.31 = (f32[2,2,64]{2,1,0:T(2,128)}, f32[2,2,64]{2,1,0:T(2,128)S(1)}, u32[]{:S(2)}) copy-start(f32[2,2,64]{2,1,0:T(2,128)S(1)} %get-tuple-element.637) | copy-start | bytes 3076
  24.1 352.7 %copy-start.33 = (f32[2,2,64]{2,1,0:T(2,128)}, f32[2,2,64]{2,1,0:T(2,128)S(1)}, u32[]{:S(2)}) copy-start(f32[2,2,64]{2,1,0:T(2,128)S(1)} %get-tuple-element.638) | copy-start | bytes 3076
  24.1 352.7 %copy-start.35 = (f32[2,2,64]{2,1,0:T(2,128)}, f32[2,2,64]{2,1,0:T(2,128)S(1)}, u32[]{:S(2)}) copy-start(f32[2,2,64]{2,1,0:T(2,128)S(1)} %get-tuple-element.639) | copy-start | bytes 3076
  24.1 352.7 %copy-start.37 = (f32[2,2,64]{2,1,0:T(2,128)}, f32[2,2,64]{2,1,0:T(2,128)S(1)}, u32[]{:S(2)}) copy-start(f32[2,2,64]{2,1,0:T(2,128)S(1)} %get-tuple-element.849) | copy-start | bytes 3076
  24.2 352.7 %copy-start.39 = (f32[2,2,64]{2,1,0:T(2,128)}, f32[2,2,64]{2,1,0:T(2,128)S(1)}, u32[]{:S(2)}) copy-start(f32[2,2,64]{2,1,0:T(2,128)S(1)} %get-tuple-element.850) | copy-start | bytes 3076
  24.2 352.7 %copy-start.41 = (f32[2,2,64]{2,1,0:T(2,128)}, f32[2,2,64]{2,1,0:T(2,128)S(1)}, u32[]{:S(2)}) copy-start(f32[2,2,64]{2,1,0:T(2,128)S(1)} %get-tuple-element.851) | copy-start | bytes 3076
  24.2 352.7 %copy-start.43 = (f32[2,2,64]{2,1,0:T(2,128)}, f32[2,2,64]{2,1,0:T(2,128)S(1)}, u32[]{:S(2)}) copy-start(f32[2,2,64]{2,1,0:T(2,128)S(1)} %get-tuple-element.852) | copy-start | bytes 3076
  27.4 10.7 collective-permute-start.2
  67.6 257.8 %collective-permute-start.3 = (f32[3,3,1,64,128]{4,3,2,1,0:T(8,128)}, f32[3,3,1,64,128]{4,3,2,1,0:T(8,128)}, u32[]{:S(2)}, u32[]{:S(2)}) collective-permute-start(f32[3,3,1,64,128]{4,3,2,1,0:T(8,128)} %get-tuple-element.168), channel_id=1, source_target_pairs={{0,1},{1,2},{2,3},{3,4},{4,5},{5,6},{6,7},{7,8},{8,9},{9,10},{10,1... | collective-permute-start | bytes 884744 | tf_op jit(solution)/shard_map/ppermute | solution.py:18
  72.5 254.0 %collective-permute-start.4 = (f32[3,3,1,64,128]{4,3,2,1,0:T(8,128)}, f32[3,3,1,64,128]{4,3,2,1,0:T(8,128)S(1)}, u32[]{:S(2)}, u32[]{:S(2)}) collective-permute-start(f32[3,3,1,64,128]{4,3,2,1,0:T(8,128)} %get-tuple-element.167), channel_id=1, source_target_pairs={{1,0},{2,1},{3,2},{4,3},{5,4},{6,5},{7,6},{8,7},{9,8},{10,9},{11,1... | collective-permute-start | bytes 884744 | tf_op jit(solution)/shard_map/ppermute | solution.py:21
  75.8 561.9 %all-reduce.63.cloned.1.call-start = ((), (), s32[]{:S(2)}) async-start(), calls=%async_computation | async-start | bytes 131072 | tf_op jit(solution)/shard_map/psum | solution.py:151
  326.6 13.3 collective-permute-start.5
  340.2 13.3 collective-permute-start.6
  342.6 18.3 %collective-permute-start.7 = (f32[3,2,1,64,128]{4,3,2,1,0:T(8,128)S(1)}, f32[3,2,1,64,128]{4,3,2,1,0:T(8,128)S(1)}, u32[]{:S(2)}, u32[]{:S(2)}) collective-permute-start(f32[3,2,1,64,128]{4,3,2,1,0:T(8,128)S(1)} %get-tuple-element.415), channel_id=1, source_target_pairs={{1,0},{2,1},{3,2},{4,3},{5,4},{6,5},{7,6},{8,7},{9,8},{10,9},{11,1... | collective-permute-start | bytes 589832 | tf_op jit(solution)/shard_map/ppermute | solution.py:21
  355.3 10.3 collective-permute-start.9
  359.0 8.0 collective-permute-start.10
  360.9 11.8 collective-permute-start.8
  367.1 10.5 collective-permute-start.11
  379.8 333.4 %all-reduce.65.cloned.1.call-start = ((), (), s32[]{:S(2)}) async-start(), calls=%async_computation.1 | async-start | bytes 131072 | tf_op jit(solution)/shard_map/psum | solution.py:151
  637.8 421.4 %all-reduce.69.cloned.1.call-start = ((), (), s32[]{:S(2)}) async-start(), calls=%async_computation.3 | async-start | bytes 131072 | tf_op jit(solution)/shard_map/psum | solution.py:139
  739.0 11.2 collective-permute-start.12
  747.5 7.0 collective-permute-start.13
  754.5 6.8 collective-permute-start.14
  790.7 19.5 %collective-permute-start.15 = (f32[3,3,1,64,128]{4,3,2,1,0:T(8,128)}, f32[3,3,1,64,128]{4,3,2,1,0:T(8,128)}, u32[]{:S(2)}, u32[]{:S(2)}) collective-permute-start(f32[3,3,1,64,128]{4,3,2,1,0:T(8,128)} %get-tuple-element.164), channel_id=1, source_target_pairs={{0,1},{1,2},{2,3},{3,4},{4,5},{5,6},{6,7},{7,8},{8,9},{9,10},{10,1... | collective-permute-start | bytes 884744 | tf_op jit(solution)/shard_map/ppermute | solution.py:18
  806.7 8.3 collective-permute-start.16
  810.1 249.0 %copy-start.3 = (f32[1,128,128]{1,2,0:T(8,128)S(1)}, f32[1,128,128]{1,2,0:T(8,128)}, u32[]{:S(2)}) copy-start(f32[1,128,128]{1,2,0:T(8,128)} %custom-call.15) | copy-start | bytes 196612
  810.1 552.0 %all-reduce.71.cloned.1.call-start = ((), (), s32[]{:S(2)}) async-start(), calls=%async_computation.4 | async-start | bytes 131072 | tf_op jit(solution)/shard_map/psum | solution.py:151
  816.1 244.5 %collective-permute-start.17 = (f32[3,1,2,64,128]{4,3,2,1,0:T(8,128)S(1)}, f32[3,1,2,64,128]{4,3,2,1,0:T(8,128)S(1)}, u32[]{:S(2)}, u32[]{:S(2)}) collective-permute-start(f32[3,1,2,64,128]{4,3,2,1,0:T(8,128)S(1)} %slice.4621), channel_id=1, source_target_pairs={{32,0},{64,32},{96,64},{128,96},{160,128},{192,160},{224,192},{33,... | collective-permute-start | bytes 589832 | tf_op jit(solution)/shard_map/ppermute | solution.py:29
  1072.1 5.1 collective-permute-start.18
  1074.6 10.8 collective-permute-start.19
  1079.1 9.5 collective-permute-start.21
  1083.5 8.0 collective-permute-start.22
  1085.5 9.5 collective-permute-start.20
  1091.7 8.3 collective-permute-start.23
  1100.7 361.6 %copy-start.2 = (f32[128,128]{1,0:T(8,128)S(1)}, f32[128,128]{1,0:T(8,128)}, u32[]{:S(2)}) copy-start(f32[128,128]{1,0:T(8,128)} %all-reduce.69.cloned.1.call-done) | copy-start | bytes 196612
  1102.2 335.5 %all-reduce.73.cloned.1.call-start = ((), (), s32[]{:S(2)}) async-start(), calls=%async_computation.5 | async-start | bytes 131072 | tf_op jit(solution)/shard_map/psum | solution.py:151
  (261 other events, 1226.2 us)
Sparse Core Ops, SparseCore 0:
  75.9 248.4 all-reduce.66
  810.3 248.8 all-reduce.68
Sparse Core Ops, SparseCore 1:
  379.9 257.8 all-reduce.62
  640.2 72.9 all-reduce.64
  1102.3 259.8 all-reduce.70
  1364.7 72.9 all-reduce.72
